TPU v7x, 256 devices: a whole 4x4x8 slice. The times are simulated.
256 devices in a mesh: slab: 4 (over y), pencil: 64 (over z, x, core).
Axes of the slice: x: 4, y: 4, z: 8, core: 2. Of those that a mesh axis runs over, the one named last changes fastest.
Arguments:
- spectrum: float32 [2, 8, 2048, 4096], P(None, 'slab', 'pencil'), may hold values from -6 to 6
Outputs:
- rendered: float32 [4, 8, 4096], P(None, 'slab', 'pencil')
All inputs are finite; a program needn't handle non-finite values.
Results may differ from a plain program's by a relative error of at most 0.0003.
Values sent between devices are 32-bit elements; how exact they have to be, the bound alone decides.
No kernel may reach another device: no remote copies, remote signals or barrier semaphores. Data moves between devices by JAX's collectives and lax.ppermute only.
A program may use at most 64 MiB of HBM per device.

v0:
```python
import math

import numpy as np

import jax
import jax.numpy as jnp
from jax import lax
from jax.experimental import pallas as pl
from jax.experimental.pallas import tpu as pltpu
from jax.sharding import PartitionSpec as P

N = 4096
AXES = ("slab", "pencil")
F32 = jnp.float32
BF16 = jnp.bfloat16


def split_np(table):
    high = table.astype(np.float32).astype(BF16)
    low = (table - high.astype(np.float64)).astype(np.float32).astype(BF16)
    return high, low


def split(value):
    high = value.astype(BF16)
    low = (value - high.astype(F32)).astype(BF16)
    return high, low


def complex_block(phase):
    cosine, sine = np.cos(phase), np.sin(phase)
    return np.block([[cosine, -sine], [sine, cosine]])


def x_tables():
    blocks = np.arange(256)
    matrix = complex_block(2 * np.pi * (blocks[:, None] * blocks[None, :] % 256) / 256)
    fine = 2 * np.pi * (np.arange(16)[:, None] * blocks[None, :] % N) / N
    twist = np.stack([np.cos(fine), np.sin(fine)], axis=1).reshape(32, 256) / 64
    return (twist.astype(np.float32),) + split_np(matrix)


def z_tables():
    outer = np.arange(128)[:, None] * np.arange(64)[None, :]
    first = complex_block(2 * np.pi * (outer % 128) / 128) / 32
    fine = 2 * np.pi * (np.arange(128)[:, None] * (np.arange(128) % 32)[None, :] % N) / N
    twist = np.stack([np.cos(fine), np.sin(fine)])
    short = 2 * np.pi * (np.arange(32)[:, None] * np.arange(32)[None, :] % 32) / 32
    second = np.concatenate(
        [np.kron(np.eye(4), np.cos(short)), -np.kron(np.eye(4), np.sin(short))], axis=1
    )
    first_high, first_low = split_np(first)
    first_both = np.concatenate([first_high, first_high], axis=1)
    return (first_both, first_low, twist.astype(np.float32)) + split_np(second)


def four(a, b, c, d):
    (ar, ai), (br, bi), (cr, ci), (dr, di) = a, b, c, d
    er, ei, fr, fi = ar + cr, ai + ci, ar - cr, ai - ci
    gr, gi, hr, hi = br + dr, bi + di, br - dr, bi - di
    return [(er + gr, ei + gi), (fr - hi, fi + hr), (er - gr, ei - gi), (fr + hi, fi - hr)]


def turned(value, steps):
    re, im = value
    if steps == 0:
        return value
    if steps == 4:
        return (-im, re)
    half = math.sqrt(0.5)
    if steps == 2:
        return ((re - im) * half, (re + im) * half)
    if steps == 6:
        return ((-re - im) * half, (re - im) * half)
    c, s = math.cos(math.pi * steps / 8), math.sin(math.pi * steps / 8)
    return (re * c - im * s, re * s + im * c)


def x_kernel(data, twist, high_w, low_w, out, high_t, low_t):
    for y in range(2):
        for half in range(2):
            for tile in range(2):
                rows = pl.ds(16 * half, 16)
                cells = [
                    tuple(
                        data[part, y, rows, pl.ds(256 * t + 128 * tile, 128)] for part in range(2)
                    )
                    for t in range(16)
                ]
                middle = [four(*(cells[4 * t1 + t0] for t1 in range(4))) for t0 in range(4)]
                for k1 in range(4):
                    ends = four(*(turned(middle[t0][k1], t0 * k1) for t0 in range(4)))
                    for k0 in range(4):
                        fine = k1 + 4 * k0
                        re, im = ends[k0]
                        lanes = pl.ds(128 * tile, 128)
                        c = twist[pl.ds(2 * fine, 1), lanes]
                        s = twist[pl.ds(2 * fine + 1, 1), lanes]
                        for part, value in enumerate((re * c - im * s, re * s + im * c)):
                            high, low = split(value)
                            at = pl.ds(64 * (fine // 8) + 32 * y + 16 * half, 16)
                            columns = pl.ds(256 * part + 128 * tile, 128)
                            high_t[fine % 8, at, columns] = high
                            low_t[fine % 8, at, columns] = low

    def send(fine, carry):
        high, low = high_t[fine], low_t[fine]
        for part in range(2):
            w_rows = pl.ds(256 * part, 256)
            value = across(high_w[w_rows], high) + across(high_w[w_rows], low)
            value = value + across(low_w[w_rows], high)
            out[pl.ds(8 * part + fine, 256, stride=16), :] = value
        return carry

    lax.fori_loop(0, 8, send, 0)


def across(left, right):
    return lax.dot_general(left, right, (((1,), (1,)), ((), ())), preferred_element_type=F32)


def straight(left, right):
    return lax.dot_general(left, right, (((1,), (0,)), ((), ())), preferred_element_type=F32)


def z_kernel(got, first_both, first_low, twist, second_high, second_low, out, field):
    lane = lax.broadcasted_iota(jnp.int32, (64, 128), 1)
    mode = lax.broadcasted_iota(jnp.int32, (64, 128), 0)
    weight = jnp.where((mode == 0) & (lane % 32 == 0), 0.5, 1.0).astype(F32)

    def transform(slab, carry):
        for pair in range(4):
            parts = []
            for part in range(2):
                parts.append(
                    jnp.concatenate(
                        [
                            got[pl.ds(slab * 1024 + 8 * part + 2 * pair + k, 64, stride=16), :]
                            * weight
                            for k in range(2)
                        ],
                        axis=1,
                    )
                )
            high, low = split(jnp.concatenate(parts, axis=0))
            lines = straight(first_both[...], jnp.concatenate([high, low], axis=0))
            lines = lines + straight(first_low[...], high)
            c, s = twist[0], twist[1]
            turned_parts = []
            for k in range(2):
                re = lines[:128, 128 * k : 128 * k + 128]
                im = lines[128:, 128 * k : 128 * k + 128]
                turned_parts.append(jnp.concatenate([re * c - im * s, re * s + im * c], axis=1))
            high, low = split(jnp.concatenate(turned_parts, axis=0))
            value = across(second_high[...], high) + across(second_high[...], low)
            value = value + across(second_low[...], high)
            for k in range(2):
                for far in range(2):
                    for y in range(2):
                        row = 64 * far + 32 * y
                        field[8 * far + 2 * pair + k, 2 * slab + y] = value[
                            row : row + 32, 128 * k : 128 * k + 128
                        ]
        return carry

    lax.fori_loop(0, 4, transform, 0)
    first_half = lax.broadcasted_iota(jnp.int32, (32, 128), 1) < 64

    def render(slab, carry):
        planes = []
        for odd in range(2):
            y = 2 * slab + odd
            before, after = (y + 7) % 8, (y + 1) % 8
            zero = jnp.zeros((32, 128), F32)
            clear, depth, total, tilted, glow = jnp.ones((32, 128), F32), zero, zero, zero, zero
            for x in range(16):
                value = field[x, y]
                shading = 1.0 + 0.5 * jnp.tanh(0.5 * (field[x, after] - field[x, before]))
                square = value * value
                extinction = square * (1.0 / N)
                passed = jnp.exp(-extinction)
                weight = clear * (1.0 - passed) * shading
                clear = clear * passed
                depth = depth + extinction
                total = total + weight
                tilted = tilted + weight * jnp.tanh(1.5 * value)
                glow = glow + weight * jnp.exp(-square)
            red = 0.5 * (total + tilted)
            planes.append((red, 0.5 * glow, total - red, depth))
        for channel in range(4):
            low, high = planes[0][channel], planes[1][channel]
            mixed = (
                jnp.where(first_half, low, pltpu.roll(high, 64, 1)),
                jnp.where(first_half, pltpu.roll(low, 64, 1), high),
            )
            for core in range(2):
                out[pl.ds(slab * 256 + 4 * core + channel, 32, stride=8), :] = mixed[core]
        return carry

    lax.fori_loop(0, 4, render, 0)


def blend_kernel(got, out):
    depth = got[pl.ds(3, 256, stride=4), :]
    row = lax.broadcasted_iota(jnp.int32, (256, 256), 0)
    col = lax.broadcasted_iota(jnp.int32, (256, 256), 1)
    earlier = (col < row).astype(BF16)
    high = depth.astype(BF16)
    rest = depth - high.astype(F32)
    middle = rest.astype(BF16)
    low = (rest - middle.astype(F32)).astype(BF16)
    before = straight(earlier, high) + straight(earlier, middle) + straight(earlier, low)
    clear = jnp.exp(-before)
    rows = [
        jnp.sum(clear * got[pl.ds(channel, 256, stride=4), :], axis=0, keepdims=True)
        for channel in range(3)
    ]
    rows.append(1.0 - jnp.exp(-jnp.sum(depth, axis=0, keepdims=True)))
    for channel in range(4):
        for y in range(2):
            out[channel, pl.ds(y, 1), :] = rows[channel][:, 64 * y : 64 * y + 64]


def vmem_call(kernel, out_shape, scratch=()):
    return pl.pallas_call(
        kernel, out_shape=jax.ShapeDtypeStruct(out_shape, F32), scratch_shapes=scratch
    )


def local(spectrum):
    tables = [jnp.asarray(table) for table in x_tables()]
    sent = vmem_call(
        x_kernel,
        (4096, 128),
        [pltpu.VMEM((8, 128, 512), BF16), pltpu.VMEM((8, 128, 512), BF16)],
    )(spectrum, *tables)
    got = lax.all_to_all(sent.reshape(256, 16, 128), AXES, split_axis=0, concat_axis=0, tiled=True)
    tables = [jnp.asarray(table) for table in z_tables()]
    sent = vmem_call(z_kernel, (1024, 128), [pltpu.VMEM((16, 8, 32, 128), F32)])(
        got.reshape(4096, 128), *tables
    )
    got = lax.all_to_all(sent.reshape(256, 4, 128), AXES, split_axis=0, concat_axis=0, tiled=True)
    return vmem_call(blend_kernel, (4, 2, 64))(got.reshape(1024, 128))


def solution(mesh):
    return jax.shard_map(
        local,
        mesh=mesh,
        in_specs=(P(None, "slab", "pencil", None),),
        out_specs=P(None, "slab", "pencil"),
        check_vma=False,
    )
```

profile of v0, /device:TPU:1, one launch (start us, length us, event | category | flops | bytes accessed | tf_op | source)
XLA Modules:
  0.0 118.4 jit_solution(17510867600646771179)
XLA Ops:
  0.0 8.9 %shard_map.91 = f32[4096,128]{1,0:T(8,128)} custom-call(f32[2,2,32,4096]{3,2,1,0:T(8,128)} %data.1, f32[32,256]{1,0:T(8,128)} %constant.16.clone.twist, bf16[512,512]{1,0:T(8,128)(2,1)} %constant.17.clone.high_w, bf16[512,512]{1,0:T(8,128)(2,1)} %constant.18.clone.low_w), custom_call_target="tpu_custom_call" | custom-call | tf_op jit(solution)/shard_map/pallas_call | solution.py:232
  8.9 69.1 %all_to_all.10 = f32[256,16,128]{2,1,0:T(8,128)} all-to-all(f32[256,16,128]{2,1,0:T(8,128)} %bitcast.5), channel_id=1, replica_groups=mesh['slab'=4,'pencil'=64] {'slab','pencil'}, dimensions={0} | all-to-all | bytes 4194304 | tf_op jit(solution)/shard_map/all_to_all | solution.py:237
  78.0 10.7 %shard_map.92 = f32[1024,128]{1,0:T(8,128)} custom-call(f32[4096,128]{1,0:T(8,128)} %bitcast.4, bf16[256,256]{1,0:T(8,128)(2,1)} %constant.19.clone.first_both, bf16[256,128]{1,0:T(8,128)(2,1)} %constant.20.clone.first_low, f32[2,128,128]{2,1,0:T(8,128)} %constant.21.clone.twist, bf16[128,256]{1,0:T(8,128)(2,1)} %constant.22.clone.second_high, ...), custom_call_target="tpu_custom_call" | custom-call | tf_op jit(solution)/shard_map/pallas_call | solution.py:239
  88.7 27.8 %all_to_all.11 = f32[256,4,128]{2,1,0:T(4,128)} all-to-all(f32[256,4,128]{2,1,0:T(4,128)} %bitcast.7), channel_id=1, replica_groups=mesh['slab'=4,'pencil'=64] {'slab','pencil'}, dimensions={0} | all-to-all | bytes 1048576 | tf_op jit(solution)/shard_map/all_to_all | solution.py:242
  116.5 2.0 %shard_map.93 = f32[4,2,64]{2,1,0:T(2,128)} custom-call(f32[1024,128]{1,0:T(8,128)} %bitcast.6), custom_call_target="tpu_custom_call" | custom-call | tf_op jit(solution)/shard_map/pallas_call | solution.py:243
where the time goes:
time: 119 us; the launch traced here: 118 us
  blocking collectives  96.9 us (81%)
  Pallas kernels  21.6 us (18%)
    all_to_all x1, blocking collectives, local(): lax.all_to_all(sent.reshape(256, 16, 128), AXES, split_axis=0, concat_axi...  69.1 us
    all_to_all x1, blocking collectives, local(): lax.all_to_all(sent.reshape(256, 4, 128), AXES, split_axis=0, concat_axis...  27.8 us
    pallas_call x1, Pallas kernels, local(): vmem_call(z_kernel, (1024, 128), [pltpu.VMEM((16, 8, 32, 128), F32)])  10.7 us
    pallas_call x1, Pallas kernels, local(): vmem_call(x_kernel, (4096, 128), [pltpu.VMEM((8, 128, 512), BF16), pltpu....  8.93 us

commit v1 on v0

v1 whole, which is shorter than its diff:
```python
import math

import numpy as np

import jax
import jax.numpy as jnp
from jax import lax
from jax.experimental import pallas as pl
from jax.experimental.pallas import tpu as pltpu
from jax.sharding import PartitionSpec as P

N = 4096
LOG2E = math.log2(math.e)
AXES = ("slab", "pencil")
F32 = jnp.float32
BF16 = jnp.bfloat16


def split_np(table):
    high = table.astype(np.float32).astype(BF16)
    low = (table - high.astype(np.float64)).astype(np.float32).astype(BF16)
    return high, low


def split(value):
    high = value.astype(BF16)
    low = (value - high.astype(F32)).astype(BF16)
    return high, low


def complex_block(phase):
    cosine, sine = np.cos(phase), np.sin(phase)
    return np.block([[cosine, -sine], [sine, cosine]])


def x_tables():
    blocks = np.arange(256)
    matrix = complex_block(2 * np.pi * (blocks[:, None] * blocks[None, :] % 256) / 256)
    fine = 2 * np.pi * (np.arange(16)[:, None] * blocks[None, :] % N) / N
    twist = np.stack([np.cos(fine), np.sin(fine)], axis=1).reshape(32, 256)
    return (twist.astype(np.float32),) + split_np(matrix)


def z_tables():
    outer = np.arange(128)[:, None] * np.arange(64)[None, :]
    first = complex_block(2 * np.pi * (outer % 128) / 128) / 4096
    fine = 2 * np.pi * (np.arange(128)[:, None] * (np.arange(128) % 32)[None, :] % N) / N
    twist = np.stack([np.cos(fine), np.sin(fine)])
    short = 2 * np.pi * (np.arange(32)[:, None] * np.arange(32)[None, :] % 32) / 32
    second = np.concatenate(
        [np.kron(np.eye(4), np.cos(short)), -np.kron(np.eye(4), np.sin(short))], axis=1
    )
    first_high, first_low = split_np(first)
    first_both = np.concatenate([first_high, first_high], axis=1)
    second_all = np.concatenate(split_np(second), axis=0)
    return (first_both, first_low, twist.astype(np.float32), second_all)


def four(a, b, c, d):
    (ar, ai), (br, bi), (cr, ci), (dr, di) = a, b, c, d
    er, ei, fr, fi = ar + cr, ai + ci, ar - cr, ai - ci
    gr, gi, hr, hi = br + dr, bi + di, br - dr, bi - di
    return [(er + gr, ei + gi), (fr - hi, fi + hr), (er - gr, ei - gi), (fr + hi, fi - hr)]


def turned(value, steps):
    re, im = value
    if steps == 0:
        return value
    if steps == 4:
        return (-im, re)
    half = math.sqrt(0.5)
    if steps == 2:
        return ((re - im) * half, (re + im) * half)
    if steps == 6:
        return ((-re - im) * half, (re - im) * half)
    c, s = math.cos(math.pi * steps / 8), math.sin(math.pi * steps / 8)
    return (re * c - im * s, re * s + im * c)


def x_kernel(
    data, twist_hbm, high_hbm, low_hbm, out, cells_v, twist, high_w, low_w, high_t, low_t, sems
):
    copies = [pltpu.make_async_copy(twist_hbm, twist, sems.at[0])]
    for y in range(2):
        for half in range(2):
            rows = pl.ds(16 * half, 16)
            copies.append(
                pltpu.make_async_copy(
                    data.at[:, y, rows, :], cells_v.at[:, y, rows, :], sems.at[1 + 2 * y + half]
                )
            )
    copies.append(pltpu.make_async_copy(high_hbm, high_w, sems.at[5]))
    copies.append(pltpu.make_async_copy(low_hbm, low_w, sems.at[6]))
    for copy in copies:
        copy.start()

    def stage(y, half, tile):
        rows, lanes = pl.ds(16 * half, 16), pl.ds(128 * tile, 128)
        cells = [
            tuple(cells_v[part, y, rows, pl.ds(256 * t + 128 * tile, 128)] for part in range(2))
            for t in range(16)
        ]
        middle = [four(*(cells[4 * t1 + t0] for t1 in range(4))) for t0 in range(4)]
        for k1 in range(4):
            ends = four(*(turned(middle[t0][k1], t0 * k1) for t0 in range(4)))
            for k0 in range(4):
                fine = k1 + 4 * k0
                value = ends[k0]
                if fine:
                    re, im = value
                    c = twist[pl.ds(2 * fine, 1), lanes]
                    s = twist[pl.ds(2 * fine + 1, 1), lanes]
                    value = (re * c - im * s, re * s + im * c)
                for part in range(2):
                    high, low = split(value[part])
                    at = pl.ds(32 * fine + 16 * half, 16)
                    columns = pl.ds(256 * part + 128 * tile, 128)
                    high_t[y, at, columns] = high
                    low_t[y, at, columns] = low

    def send(y, pair, part):
        rows, w_rows = pl.ds(256 * pair, 256), pl.ds(256 * part, 256)
        high, low = high_t[y, rows], low_t[y, rows]
        value = across(high_w[w_rows], high) + across(low_w[w_rows], high)
        value = value + across(high_w[w_rows], low)
        for k in range(2):
            row = 8 * part + 4 * y + 2 * pair + k
            out[pl.ds(row, 256, stride=16), :] = value[:, 128 * k : 128 * k + 128]

    copies[0].wait()
    for half in range(2):
        copies[1 + half].wait()
        for tile in range(2):
            stage(0, half, tile)
    for copy in copies[3:]:
        copy.wait()
    for first in range(2):
        for second in range(2):
            send(0, first, second)
            stage(1, first, second)
    for pair in range(2):
        for part in range(2):
            send(1, pair, part)


def across(left, right):
    return lax.dot_general(left, right, (((1,), (1,)), ((), ())), preferred_element_type=F32)


def straight(left, right):
    return lax.dot_general(left, right, (((1,), (0,)), ((), ())), preferred_element_type=F32)


def z_kernel(got, first_both, first_low, twist, second_all, out, field, high_q, low_q, image):
    lane = lax.broadcasted_iota(jnp.int32, (8, 128), 1)
    mode = lax.broadcasted_iota(jnp.int32, (8, 128), 0)
    weight = jnp.where((mode == 0) & (lane % 32 == 0), 0.5, 1.0).astype(F32)

    def first(slab, y, pair, slot):
        parts = []
        for part in range(2):
            blocks = []
            for k in range(2):
                row = slab * 1024 + 8 * part + 4 * y + 2 * pair + k
                head = got[pl.ds(row, 8, stride=16), :] * weight
                blocks.append(
                    jnp.concatenate([head, got[pl.ds(row + 128, 56, stride=16), :]], axis=0)
                )
            parts.append(jnp.concatenate(blocks, axis=1))
        high, low = split(jnp.concatenate(parts, axis=0))
        both = jnp.concatenate([high, low], axis=0)
        for part in range(2):
            half = pl.ds(64 * part, 64)
            other = pl.ds(128 + 64 * part, 64)
            re = straight(first_both[half], both) + straight(first_low[half], high)
            im = straight(first_both[other], both) + straight(first_low[other], high)
            c, s = twist[0, half], twist[1, half]
            for k in range(2):
                r, i = re[:, 128 * k : 128 * k + 128], im[:, 128 * k : 128 * k + 128]
                at = pl.ds(128 * k + 64 * part, 64)
                for column, value in enumerate((r * c - i * s, r * s + i * c)):
                    high_q[slot, at, pl.ds(128 * column, 128)], low_q[
                        slot, at, pl.ds(128 * column, 128)
                    ] = split(value)

    def second(slab, y, pair, slot):
        value = across(second_all[pl.ds(0, 128)], high_q[slot])
        value = value + across(second_all[pl.ds(128, 128)], high_q[slot])
        value = value + across(second_all[pl.ds(0, 128)], low_q[slot])
        for k in range(2):
            for near in range(4):
                field[4 * (2 * pair + k) + near, 2 * slab + y] = value[
                    32 * near : 32 * near + 32, 128 * k : 128 * k + 128
                ]

    first(0, 0, 0, 0)

    def transform(step, carry):
        slab, y = step // 2, step % 2
        after = jnp.minimum(step + 1, 7)
        first(slab, y, 1, 1)
        second(slab, y, 0, 0)
        first(after // 2, after % 2, 0, 0)
        second(slab, y, 1, 1)
        return carry

    lax.fori_loop(0, 8, transform, 0)

    def render(y, carry):
        before, after = (y + 7) % 8, (y + 1) % 8
        zero = jnp.zeros((32, 128), F32)
        clear, depth, total, tilted, glow = jnp.ones((32, 128), F32), zero, zero, zero, zero
        for x in range(16):
            half = field[x, y]
            shading = 2.0 + jnp.tanh(field[x, after] - field[x, before])
            square = half * half
            passed = jnp.exp2(square * (-4.0 * LOG2E / N))
            weight = (clear * shading) * (1.0 - passed)
            clear = clear * passed
            depth = depth + square
            total = total + weight
            tilted = tilted + weight * jnp.tanh(3.0 * half)
            glow = glow + weight * jnp.exp2(square * (-4.0 * LOG2E))
        red = 0.25 * (total + tilted)
        image[0, y] = red
        image[1, y] = 0.25 * glow
        image[2, y] = 0.5 * total - red
        image[3, y] = depth * (4.0 / N)
        return carry

    lax.fori_loop(0, 8, render, 0)
    first_half = lax.broadcasted_iota(jnp.int32, (32, 128), 1) < 64
    for slab in range(4):
        for channel in range(4):
            low, high = image[channel, 2 * slab], image[channel, 2 * slab + 1]
            mixed = (
                jnp.where(first_half, low, pltpu.roll(high, 64, 1)),
                jnp.where(first_half, pltpu.roll(low, 64, 1), high),
            )
            for core in range(2):
                out[pl.ds(slab * 256 + 4 * core + channel, 32, stride=8), :] = mixed[core]


def blend_kernel(got, out):
    depth = got[pl.ds(3, 256, stride=4), :]
    row = lax.broadcasted_iota(jnp.int32, (256, 256), 0)
    col = lax.broadcasted_iota(jnp.int32, (256, 256), 1)
    earlier = (col < row).astype(BF16)
    high = depth.astype(BF16)
    rest = depth - high.astype(F32)
    middle = rest.astype(BF16)
    low = (rest - middle.astype(F32)).astype(BF16)
    before = straight(earlier, high) + straight(earlier, middle) + straight(earlier, low)
    clear = jnp.exp(-before)
    rows = [
        jnp.sum(clear * got[pl.ds(channel, 256, stride=4), :], axis=0, keepdims=True)
        for channel in range(3)
    ]
    rows.append(1.0 - jnp.exp(-jnp.sum(depth, axis=0, keepdims=True)))
    for channel in range(4):
        for y in range(2):
            out[channel, pl.ds(y, 1), :] = rows[channel][:, 64 * y : 64 * y + 64]


def vmem_call(kernel, out_type, scratch=(), in_specs=None):
    params = pltpu.CompilerParams(vmem_limit_bytes=24 << 20)
    specs = {} if in_specs is None else {"in_specs": in_specs}
    return pl.pallas_call(
        kernel, out_shape=out_type, scratch_shapes=scratch, compiler_params=params, **specs
    )


def exchanged(blocks):
    got = lax.all_to_all(blocks, AXES, split_axis=0, concat_axis=0, tiled=True)
    return pltpu.with_memory_space_constraint(got.reshape(-1, 128), pltpu.VMEM)


def pinned(array):
    return pltpu.with_memory_space_constraint(array, pltpu.HBM)


def x_call(spectrum):
    tables = [pinned(jnp.asarray(table)) for table in x_tables()]
    far = pl.BlockSpec(memory_space=pltpu.HBM)
    lines = pltpu.VMEM((2, 512, 512), BF16)
    matrix = pltpu.VMEM((512, 512), BF16)
    return vmem_call(
        x_kernel,
        pltpu.VMEM((4096, 128), F32),
        [
            pltpu.VMEM((2, 2, 32, 4096), F32),
            pltpu.VMEM((32, 256), F32),
            matrix,
            matrix,
            lines,
            lines,
            pltpu.SemaphoreType.DMA((7,)),
        ],
        [far] * 4,
    )(pinned(spectrum), *tables)


def z_call(got):
    tables = [jnp.asarray(table) for table in z_tables()]
    lines = pltpu.VMEM((2, 256, 256), BF16)
    return vmem_call(
        z_kernel,
        pltpu.VMEM((1024, 128), F32),
        [pltpu.VMEM((16, 8, 32, 128), F32), lines, lines, pltpu.VMEM((4, 8, 32, 128), F32)],
    )(got, *tables)


def local(spectrum):
    got = exchanged(x_call(spectrum).reshape(256, 16, 128))
    got = exchanged(z_call(got).reshape(256, 4, 128))
    return vmem_call(blend_kernel, jax.ShapeDtypeStruct((4, 2, 64), F32))(got)


def solution(mesh):
    return jax.shard_map(
        local,
        mesh=mesh,
        in_specs=(P(None, "slab", "pencil", None),),
        out_specs=P(None, "slab", "pencil"),
        check_vma=False,
    )
```

time: 119 us -> 109 us (0.916)
  Pallas kernels: 21.6 us -> 13.1 us
  blocking collectives: 96.9 us -> 95.5 us
    pallas_call x3, Pallas kernels: 21.6 us -> 13.1 us  [the longest x1 7.82 us: z_call(): vmem_call(z_kernel, pltpu.VMEM((1024, 128), F32), [pltpu.VMEM((16, 8, 32,...]
    all_to_all x2, blocking collectives: 96.9 us -> 95.5 us  [exchanged(): got = lax.all_to_all(blocks, AXES, split_axis=0, concat_axis=0, tiled=True)]
where the time goes in v1:
time: 109 us
  blocking collectives  95.5 us (88%)
  Pallas kernels  13.1 us (12%)
    all_to_all x2, blocking collectives, exchanged(): got = lax.all_to_all(blocks, AXES, split_axis=0, concat_axis=0, tiled=True)  95.5 us
    pallas_call x1, Pallas kernels, z_call(): vmem_call(z_kernel, pltpu.VMEM((1024, 128), F32), [pltpu.VMEM((16, 8, 32,...  7.82 us
    pallas_call x1, Pallas kernels, x_call(): vmem_call(x_kernel, pltpu.VMEM((4096, 128), F32), [pltpu.VMEM((2, 2, 32,...  4.34 us

profile of v1, /device:TPU:1, one launch (start us, length us, event | category | flops | bytes accessed | tf_op | source)
XLA Modules:
  0.0 108.7 jit_solution(10923377319721010712)
XLA Ops:
  0.0 4.3 %shard_map.82 = f32[4096,128]{1,0:T(8,128)S(1)} custom-call(f32[2,2,32,4096]{3,2,1,0:T(8,128)} %data.1, f32[32,256]{1,0:T(8,128)} %constant.14.clone.twist_hbm, bf16[512,512]{1,0:T(8,128)(2,1)} %constant.15.clone.high_hbm, bf16[512,512]{1,0:T(8,128)(2,1)} %constant.16.clone.low_hbm), custom_call_target="tpu_custom_call" | custom-call | tf_op jit(solution)/shard_map/pallas_call | solution.py:288
  4.3 0.0 copy-start
  4.4 0.0 copy-start.1
  4.4 0.0 copy-start.2
  4.4 0.0 copy-start.3
  4.4 68.8 %all_to_all.10 = f32[256,16,128]{2,1,0:T(8,128)S(1)} all-to-all(f32[256,16,128]{2,1,0:T(8,128)S(1)} %bitcast.5), channel_id=1, replica_groups=mesh['slab'=4,'pencil'=64] {'slab','pencil'}, dimensions={0} | all-to-all | bytes 4194304 | tf_op jit(solution)/shard_map/all_to_all | solution.py:275
  73.2 0.0 copy-done
  73.2 0.0 copy-done.1
  73.2 0.0 copy-done.2
  73.2 0.0 copy-done.3
  73.2 7.8 %shard_map.83 = f32[1024,128]{1,0:T(8,128)S(1)} custom-call(f32[4096,128]{1,0:T(8,128)S(1)} %bitcast.4, bf16[256,256]{1,0:T(8,128)(2,1)S(1)} %copy-done.2, bf16[256,128]{1,0:T(8,128)(2,1)S(1)} %copy-done.3, f32[2,128,128]{2,1,0:T(8,128)S(1)} %copy-done.1, bf16[256,256]{1,0:T(8,128)(2,1)S(1)} %copy-done), custom_call_target="tpu_custom_call" | custom-call | tf_op jit(solution)/shard_map/pallas_call | solution.py:307
  81.0 26.7 %all_to_all.11 = f32[256,4,128]{2,1,0:T(4,128)S(1)} all-to-all(f32[256,4,128]{2,1,0:T(4,128)S(1)} %bitcast.7), channel_id=1, replica_groups=mesh['slab'=4,'pencil'=64] {'slab','pencil'}, dimensions={0} | all-to-all | bytes 1048576 | tf_op jit(solution)/shard_map/all_to_all | solution.py:275
  107.7 0.9 shard_map.84
Async XLA Ops:
  4.3 68.8 %copy-start = (bf16[256,256]{1,0:T(8,128)(2,1)S(1)}, bf16[256,256]{1,0:T(8,128)(2,1)}, u32[]{:S(2)}) copy-start(bf16[256,256]{1,0:T(8,128)(2,1)} %constant.20.clone.second_all) | copy-start | bytes 393220
  4.4 68.8 %copy-start.1 = (f32[2,128,128]{2,1,0:T(8,128)S(1)}, f32[2,128,128]{2,1,0:T(8,128)}, u32[]{:S(2)}) copy-start(f32[2,128,128]{2,1,0:T(8,128)} %constant.19.clone.twist) | copy-start | bytes 393220
  4.4 68.8 %copy-start.2 = (bf16[256,256]{1,0:T(8,128)(2,1)S(1)}, bf16[256,256]{1,0:T(8,128)(2,1)}, u32[]{:S(2)}) copy-start(bf16[256,256]{1,0:T(8,128)(2,1)} %constant.17.clone.first_both) | copy-start | bytes 393220
  4.4 68.8 %copy-start.3 = (bf16[256,128]{1,0:T(8,128)(2,1)S(1)}, bf16[256,128]{1,0:T(8,128)(2,1)}, u32[]{:S(2)}) copy-start(bf16[256,128]{1,0:T(8,128)(2,1)} %constant.18.clone.first_low) | copy-start | bytes 196612

commit v2 on v1

--- a/solution.py
+++ b/solution.py
@@ -36,6 +36,7 @@
 def x_tables():
     blocks = np.arange(256)
     matrix = complex_block(2 * np.pi * (blocks[:, None] * blocks[None, :] % 256) / 256)
+    matrix = matrix.reshape(2, 256, 512).transpose(1, 0, 2).reshape(512, 512)
     fine = 2 * np.pi * (np.arange(16)[:, None] * blocks[None, :] % N) / N
     twist = np.stack([np.cos(fine), np.sin(fine)], axis=1).reshape(32, 256)
     return (twist.astype(np.float32),) + split_np(matrix)
@@ -50,6 +51,7 @@
     second = np.concatenate(
         [np.kron(np.eye(4), np.cos(short)), -np.kron(np.eye(4), np.sin(short))], axis=1
     )
+    first = first.reshape(256, 2, 64).transpose(0, 2, 1).reshape(256, 128)
     first_high, first_low = split_np(first)
     first_both = np.concatenate([first_high, first_high], axis=1)
     second_all = np.concatenate(split_np(second), axis=0)
@@ -119,14 +121,12 @@
                     high_t[y, at, columns] = high
                     low_t[y, at, columns] = low
 
-    def send(y, pair, part):
-        rows, w_rows = pl.ds(256 * pair, 256), pl.ds(256 * part, 256)
+    def send(y, pair):
+        rows = pl.ds(256 * pair, 256)
         high, low = high_t[y, rows], low_t[y, rows]
-        value = across(high_w[w_rows], high) + across(low_w[w_rows], high)
-        value = value + across(high_w[w_rows], low)
+        value = across(high_w[...], high) + across(low_w[...], high) + across(high_w[...], low)
         for k in range(2):
-            row = 8 * part + 4 * y + 2 * pair + k
-            out[pl.ds(row, 256, stride=16), :] = value[:, 128 * k : 128 * k + 128]
+            out[pl.ds(4 * y + 2 * pair + k, 512, stride=8), :] = value[:, 128 * k : 128 * k + 128]
 
     copies[0].wait()
     for half in range(2):
@@ -135,13 +135,12 @@
             stage(0, half, tile)
     for copy in copies[3:]:
         copy.wait()
-    for first in range(2):
-        for second in range(2):
-            send(0, first, second)
-            stage(1, first, second)
     for pair in range(2):
-        for part in range(2):
-            send(1, pair, part)
+        send(0, pair)
+        for tile in range(2):
+            stage(1, pair, tile)
+    for pair in range(2):
+        send(1, pair)
 
 
 def across(left, right):
@@ -154,58 +153,53 @@
 
 def z_kernel(got, first_both, first_low, twist, second_all, out, field, high_q, low_q, image):
     lane = lax.broadcasted_iota(jnp.int32, (8, 128), 1)
-    mode = lax.broadcasted_iota(jnp.int32, (8, 128), 0)
+    mode = lax.broadcasted_iota(jnp.int32, (8, 128), 0) // 2
     weight = jnp.where((mode == 0) & (lane % 32 == 0), 0.5, 1.0).astype(F32)
 
     def first(slab, y, pair, slot):
-        parts = []
-        for part in range(2):
-            blocks = []
-            for k in range(2):
-                row = slab * 1024 + 8 * part + 4 * y + 2 * pair + k
-                head = got[pl.ds(row, 8, stride=16), :] * weight
-                blocks.append(
-                    jnp.concatenate([head, got[pl.ds(row + 128, 56, stride=16), :]], axis=0)
-                )
-            parts.append(jnp.concatenate(blocks, axis=1))
-        high, low = split(jnp.concatenate(parts, axis=0))
-        both = jnp.concatenate([high, low], axis=0)
+        blocks = []
+        for k in range(2):
+            row = slab * 1024 + 4 * y + 2 * pair + k
+            head = got[pl.ds(row, 8, stride=8), :] * weight
+            blocks.append(jnp.concatenate([head, got[pl.ds(row + 64, 120, stride=8), :]], axis=0))
+        high, low = split(jnp.concatenate(blocks, axis=1))
+        value = straight(first_both[...], jnp.concatenate([high, low], axis=0))
+        value = value + straight(first_low[...], high)
         for part in range(2):
             half = pl.ds(64 * part, 64)
-            other = pl.ds(128 + 64 * part, 64)
-            re = straight(first_both[half], both) + straight(first_low[half], high)
-            im = straight(first_both[other], both) + straight(first_low[other], high)
             c, s = twist[0, half], twist[1, half]
             for k in range(2):
-                r, i = re[:, 128 * k : 128 * k + 128], im[:, 128 * k : 128 * k + 128]
+                lanes = slice(128 * k, 128 * k + 128)
+                r = value[64 * part : 64 * part + 64, lanes]
+                i = value[128 + 64 * part : 192 + 64 * part, lanes]
                 at = pl.ds(128 * k + 64 * part, 64)
-                for column, value in enumerate((r * c - i * s, r * s + i * c)):
-                    high_q[slot, at, pl.ds(128 * column, 128)], low_q[
-                        slot, at, pl.ds(128 * column, 128)
-                    ] = split(value)
+                for column, turned_value in enumerate((r * c - i * s, r * s + i * c)):
+                    columns = pl.ds(128 * column, 128)
+                    high, low = split(turned_value)
+                    high_q[slot, at, columns] = high
+                    low_q[slot, at, columns] = low
 
     def second(slab, y, pair, slot):
-        value = across(second_all[pl.ds(0, 128)], high_q[slot])
-        value = value + across(second_all[pl.ds(128, 128)], high_q[slot])
-        value = value + across(second_all[pl.ds(0, 128)], low_q[slot])
+        both = across(second_all[...], high_q[slot])
+        value = both[:128] + both[128:] + across(second_all[pl.ds(0, 128)], low_q[slot])
         for k in range(2):
             for near in range(4):
                 field[4 * (2 * pair + k) + near, 2 * slab + y] = value[
                     32 * near : 32 * near + 32, 128 * k : 128 * k + 128
                 ]
 
-    first(0, 0, 0, 0)
-
-    def transform(step, carry):
-        slab, y = step // 2, step % 2
-        after = jnp.minimum(step + 1, 7)
-        first(slab, y, 1, 1)
-        second(slab, y, 0, 0)
-        first(after // 2, after % 2, 0, 0)
-        second(slab, y, 1, 1)
+    for pair in range(2):
+        first(0, 0, pair, pair)
+
+    def transform(slab, carry):
+        after = jnp.minimum(slab + 1, 3)
+        for y in range(2):
+            for pair in range(2):
+                first(slab if y == 0 else after, 1 - y, pair, 2 - 2 * y + pair)
+                second(slab, y, pair, 2 * y + pair)
         return carry
 
-    lax.fori_loop(0, 8, transform, 0)
+    lax.fori_loop(0, 4, transform, 0, unroll=True)
 
     def render(y, carry):
         before, after = (y + 7) % 8, (y + 1) % 8
@@ -303,7 +297,7 @@
 
 def z_call(got):
     tables = [jnp.asarray(table) for table in z_tables()]
-    lines = pltpu.VMEM((2, 256, 256), BF16)
+    lines = pltpu.VMEM((4, 256, 256), BF16)
     return vmem_call(
         z_kernel,
         pltpu.VMEM((1024, 128), F32),

time: 109 us -> 106 us (0.972)
  Pallas kernels: 13.1 us -> 9.89 us
    pallas_call x1, Pallas kernels: 7.82 us -> 4.85 us  [z_call(): vmem_call(z_kernel, pltpu.VMEM((1024, 128), F32), [pltpu.VMEM((16, 8, 32,...]
where the time goes in v2:
time: 106 us; the launch traced here: 105 us
  blocking collectives  95.5 us (90%)
  Pallas kernels  9.89 us (9%)
    all_to_all x2, blocking collectives, exchanged(): got = lax.all_to_all(blocks, AXES, split_axis=0, concat_axis=0, tiled=True)  95.5 us
    pallas_call x1, Pallas kernels, z_call(): vmem_call(z_kernel, pltpu.VMEM((1024, 128), F32), [pltpu.VMEM((16, 8, 32,...  4.85 us
    pallas_call x1, Pallas kernels, x_call(): vmem_call(x_kernel, pltpu.VMEM((4096, 128), F32), [pltpu.VMEM((2, 2, 32,...  4.1 us

profile of v2, /device:TPU:1, one launch (start us, length us, event | category | flops | bytes accessed | tf_op | source)
XLA Modules:
  0.0 105.5 jit_solution(8825482997074710228)
XLA Ops:
  0.0 4.1 %shard_map.82 = f32[4096,128]{1,0:T(8,128)S(1)} custom-call(f32[2,2,32,4096]{3,2,1,0:T(8,128)} %data.1, f32[32,256]{1,0:T(8,128)} %constant.14.clone.twist_hbm, bf16[512,512]{1,0:T(8,128)(2,1)} %constant.15.clone.high_hbm, bf16[512,512]{1,0:T(8,128)(2,1)} %constant.16.clone.low_hbm), custom_call_target="tpu_custom_call" | custom-call | tf_op jit(solution)/shard_map/pallas_call | solution.py:282
  4.1 0.0 copy-start
  4.1 0.0 copy-start.1
  4.1 0.0 copy-start.2
  4.2 0.0 copy-start.3
  4.2 68.8 %all_to_all.10 = f32[256,16,128]{2,1,0:T(8,128)S(1)} all-to-all(f32[256,16,128]{2,1,0:T(8,128)S(1)} %bitcast.5), channel_id=1, replica_groups=mesh['slab'=4,'pencil'=64] {'slab','pencil'}, dimensions={0} | all-to-all | bytes 4194304 | tf_op jit(solution)/shard_map/all_to_all | solution.py:269
  72.9 0.0 copy-done
  72.9 0.0 copy-done.1
  72.9 0.0 copy-done.2
  73.0 0.0 copy-done.3
  73.0 4.8 %shard_map.83 = f32[1024,128]{1,0:T(8,128)S(1)} custom-call(f32[4096,128]{1,0:T(8,128)S(1)} %bitcast.4, bf16[256,256]{1,0:T(8,128)(2,1)S(1)} %copy-done.2, bf16[256,128]{1,0:T(8,128)(2,1)S(1)} %copy-done.3, f32[2,128,128]{2,1,0:T(8,128)S(1)} %copy-done.1, bf16[256,256]{1,0:T(8,128)(2,1)S(1)} %copy-done), custom_call_target="tpu_custom_call" | custom-call | tf_op jit(solution)/shard_map/pallas_call | solution.py:301
  77.8 26.7 %all_to_all.11 = f32[256,4,128]{2,1,0:T(4,128)S(1)} all-to-all(f32[256,4,128]{2,1,0:T(4,128)S(1)} %bitcast.7), channel_id=1, replica_groups=mesh['slab'=4,'pencil'=64] {'slab','pencil'}, dimensions={0} | all-to-all | bytes 1048576 | tf_op jit(solution)/shard_map/all_to_all | solution.py:269
  104.5 0.9 shard_map.84
Async XLA Ops:
  4.1 68.8 %copy-start = (bf16[256,256]{1,0:T(8,128)(2,1)S(1)}, bf16[256,256]{1,0:T(8,128)(2,1)}, u32[]{:S(2)}) copy-start(bf16[256,256]{1,0:T(8,128)(2,1)} %constant.20.clone.second_all) | copy-start | bytes 393220
  4.1 68.8 %copy-start.1 = (f32[2,128,128]{2,1,0:T(8,128)S(1)}, f32[2,128,128]{2,1,0:T(8,128)}, u32[]{:S(2)}) copy-start(f32[2,128,128]{2,1,0:T(8,128)} %constant.19.clone.twist) | copy-start | bytes 393220
  4.1 68.8 %copy-start.2 = (bf16[256,256]{1,0:T(8,128)(2,1)S(1)}, bf16[256,256]{1,0:T(8,128)(2,1)}, u32[]{:S(2)}) copy-start(bf16[256,256]{1,0:T(8,128)(2,1)} %constant.17.clone.first_both) | copy-start | bytes 393220
  4.2 68.8 %copy-start.3 = (bf16[256,128]{1,0:T(8,128)(2,1)S(1)}, bf16[256,128]{1,0:T(8,128)(2,1)}, u32[]{:S(2)}) copy-start(bf16[256,128]{1,0:T(8,128)(2,1)} %constant.18.clone.first_low) | copy-start | bytes 196612

commit v3 on v2

--- a/solution.py
+++ b/solution.py
@@ -34,10 +34,11 @@
 
 
 def x_tables():
-    blocks = np.arange(256)
-    matrix = complex_block(2 * np.pi * (blocks[:, None] * blocks[None, :] % 256) / 256)
-    matrix = matrix.reshape(2, 256, 512).transpose(1, 0, 2).reshape(512, 512)
-    fine = 2 * np.pi * (np.arange(16)[:, None] * blocks[None, :] % N) / N
+    lines = np.arange(256)
+    phase = 2 * np.pi * ((2 * np.arange(128) + 1)[:, None] * lines[None, :] % 512) / 512
+    cosine, sine = np.cos(phase), np.sin(phase)
+    matrix = np.stack([[cosine, sine], [-sine, cosine]]).transpose(0, 2, 1, 3).reshape(512, 256)
+    fine = 2 * np.pi * ((np.arange(16) - 8)[:, None] * lines[None, :] % N) / N
     twist = np.stack([np.cos(fine), np.sin(fine)], axis=1).reshape(32, 256)
     return (twist.astype(np.float32),) + split_np(matrix)
 
@@ -52,8 +53,9 @@
         [np.kron(np.eye(4), np.cos(short)), -np.kron(np.eye(4), np.sin(short))], axis=1
     )
     first = first.reshape(256, 2, 64).transpose(0, 2, 1).reshape(256, 128)
+    first = np.stack([first, first * np.where(np.arange(128) % 2, -1.0, 1.0)])
     first_high, first_low = split_np(first)
-    first_both = np.concatenate([first_high, first_high], axis=1)
+    first_both = np.concatenate([first_high, first_high], axis=2)
     second_all = np.concatenate(split_np(second), axis=0)
     return (first_both, first_low, twist.astype(np.float32), second_all)
 
@@ -109,7 +111,7 @@
             for k0 in range(4):
                 fine = k1 + 4 * k0
                 value = ends[k0]
-                if fine:
+                if fine != 8:
                     re, im = value
                     c = twist[pl.ds(2 * fine, 1), lanes]
                     s = twist[pl.ds(2 * fine + 1, 1), lanes]
@@ -123,10 +125,16 @@
 
     def send(y, pair):
         rows = pl.ds(256 * pair, 256)
-        high, low = high_t[y, rows], low_t[y, rows]
-        value = across(high_w[...], high) + across(low_w[...], high) + across(high_w[...], low)
-        for k in range(2):
-            out[pl.ds(4 * y + 2 * pair + k, 512, stride=8), :] = value[:, 128 * k : 128 * k + 128]
+        parts = []
+        for part in range(2):
+            at = pl.ds(256 * part, 256)
+            high, low = high_t[y, rows, at], low_t[y, rows, at]
+            value = across(high_w[at], high) + across(low_w[at], high) + across(high_w[at], low)
+            parts.append(value)
+        for side, value in enumerate((parts[0] + parts[1], parts[0] - parts[1])):
+            for k in range(2):
+                at = pl.ds(2048 * side + 4 * y + 2 * pair + k, 256, stride=8)
+                out[at, :] = value[:, 128 * k : 128 * k + 128]
 
     copies[0].wait()
     for half in range(2):
@@ -151,7 +159,11 @@
     return lax.dot_general(left, right, (((1,), (0,)), ((), ())), preferred_element_type=F32)
 
 
-def z_kernel(got, first_both, first_low, twist, second_all, out, field, high_q, low_q, image):
+def z_kernel(
+    got, first_both, first_low, twist, second_all, keep, give, field, high_q, low_q, image
+):
+    mirrored = lax.axis_index("slab") // 2
+    core = lax.axis_index("pencil") % 2
     lane = lax.broadcasted_iota(jnp.int32, (8, 128), 1)
     mode = lax.broadcasted_iota(jnp.int32, (8, 128), 0) // 2
     weight = jnp.where((mode == 0) & (lane % 32 == 0), 0.5, 1.0).astype(F32)
@@ -163,8 +175,8 @@
             head = got[pl.ds(row, 8, stride=8), :] * weight
             blocks.append(jnp.concatenate([head, got[pl.ds(row + 64, 120, stride=8), :]], axis=0))
         high, low = split(jnp.concatenate(blocks, axis=1))
-        value = straight(first_both[...], jnp.concatenate([high, low], axis=0))
-        value = value + straight(first_low[...], high)
+        value = straight(first_both[mirrored], jnp.concatenate([high, low], axis=0))
+        value = value + straight(first_low[mirrored], high)
         for part in range(2):
             half = pl.ds(64 * part, 64)
             c, s = twist[0, half], twist[1, half]
@@ -232,15 +244,33 @@
                 jnp.where(first_half, low, pltpu.roll(high, 64, 1)),
                 jnp.where(first_half, pltpu.roll(low, 64, 1), high),
             )
-            for core in range(2):
-                out[pl.ds(slab * 256 + 4 * core + channel, 32, stride=8), :] = mixed[core]
+            at = pl.ds(32 * (4 * channel + slab), 32)
+            keep[at, :] = jnp.where(core == 0, mixed[0], mixed[1])
+            give[at, :] = jnp.where(core == 0, mixed[1], mixed[0])
+
+
+def pair_kernel(keep, got, out):
+    own_first = lax.axis_index("pencil") % 2 == lax.axis_index("slab") // 2
+    for slab in range(4):
+        own = [keep[pl.ds(32 * (4 * channel + slab), 32), :] for channel in range(4)]
+        other = [got[pl.ds(32 * (4 * channel + slab), 32), :] for channel in range(4)]
+        clear = jnp.exp(-jnp.where(own_first, own[3], other[3]))
+        for channel in range(4):
+            if channel == 3:
+                value = own[3] + other[3]
+            else:
+                front = jnp.where(own_first, own[channel], other[channel])
+                back = jnp.where(own_first, other[channel], own[channel])
+                value = front + clear * back
+            out[pl.ds(128 * slab + channel, 32, stride=4), :] = value
 
 
 def blend_kernel(got, out):
-    depth = got[pl.ds(3, 256, stride=4), :]
-    row = lax.broadcasted_iota(jnp.int32, (256, 256), 0)
-    col = lax.broadcasted_iota(jnp.int32, (256, 256), 1)
-    earlier = (col < row).astype(BF16)
+    depth = got[pl.ds(3, 128, stride=4), :]
+    row = lax.broadcasted_iota(jnp.int32, (128, 128), 0)
+    col = lax.broadcasted_iota(jnp.int32, (128, 128), 1)
+    rank = jnp.where(row < 64, row, 191 - row)
+    earlier = (jnp.where(col < 64, col, 191 - col) < rank).astype(BF16)
     high = depth.astype(BF16)
     rest = depth - high.astype(F32)
     middle = rest.astype(BF16)
@@ -248,7 +278,7 @@
     before = straight(earlier, high) + straight(earlier, middle) + straight(earlier, low)
     clear = jnp.exp(-before)
     rows = [
-        jnp.sum(clear * got[pl.ds(channel, 256, stride=4), :], axis=0, keepdims=True)
+        jnp.sum(clear * got[pl.ds(channel, 128, stride=4), :], axis=0, keepdims=True)
         for channel in range(3)
     ]
     rows.append(1.0 - jnp.exp(-jnp.sum(depth, axis=0, keepdims=True)))
@@ -265,9 +295,8 @@
     )
 
 
-def exchanged(blocks):
-    got = lax.all_to_all(blocks, AXES, split_axis=0, concat_axis=0, tiled=True)
-    return pltpu.with_memory_space_constraint(got.reshape(-1, 128), pltpu.VMEM)
+def near(array):
+    return pltpu.with_memory_space_constraint(array, pltpu.VMEM)
 
 
 def pinned(array):
@@ -278,7 +307,7 @@
     tables = [pinned(jnp.asarray(table)) for table in x_tables()]
     far = pl.BlockSpec(memory_space=pltpu.HBM)
     lines = pltpu.VMEM((2, 512, 512), BF16)
-    matrix = pltpu.VMEM((512, 512), BF16)
+    matrix = pltpu.VMEM((512, 256), BF16)
     return vmem_call(
         x_kernel,
         pltpu.VMEM((4096, 128), F32),
@@ -300,15 +329,29 @@
     lines = pltpu.VMEM((4, 256, 256), BF16)
     return vmem_call(
         z_kernel,
-        pltpu.VMEM((1024, 128), F32),
+        (pltpu.VMEM((512, 128), F32), pltpu.VMEM((512, 128), F32)),
         [pltpu.VMEM((16, 8, 32, 128), F32), lines, lines, pltpu.VMEM((4, 8, 32, 128), F32)],
     )(got, *tables)
 
 
 def local(spectrum):
-    got = exchanged(x_call(spectrum).reshape(256, 16, 128))
-    got = exchanged(z_call(got).reshape(256, 4, 128))
-    return vmem_call(blend_kernel, jax.ShapeDtypeStruct((4, 2, 64), F32))(got)
+    blocks = x_call(spectrum).reshape(256, 16, 128)
+    got = lax.all_to_all(blocks, AXES, split_axis=0, concat_axis=0, tiled=True)
+    keep, give = z_call(near(got.reshape(4096, 128)))
+    swap = [(i, i ^ 1) for i in range(lax.axis_size("pencil"))]
+    other = near(lax.ppermute(give, "pencil", swap))
+    blocks = vmem_call(pair_kernel, pltpu.VMEM((512, 128), F32))(near(keep), other)
+    same_core = [[2 * i + core for i in range(128)] for core in range(2)]
+    got = lax.all_to_all(
+        blocks.reshape(128, 4, 128),
+        AXES,
+        split_axis=0,
+        concat_axis=0,
+        axis_index_groups=same_core,
+        tiled=True,
+    )
+    out_type = jax.ShapeDtypeStruct((4, 2, 64), F32)
+    return vmem_call(blend_kernel, out_type)(near(got.reshape(512, 128)))
 
 
 def solution(mesh):

time: 106 us -> 99.8 us (0.942)
  blocking collectives: 95.5 us -> 88.4 us
  waiting for transfers between devices: 0 us -> 1.16 us
    all_to_all x2, blocking collectives: 95.5 us -> 88.4 us  [the longest x1 68.8 us: local(): got = lax.all_to_all(blocks, AXES, split_axis=0, concat_axis=0, tiled=True)]
    ppermute x0 -> x1, waiting for transfers between devices: none -> 1.16 us  [local(): other = near(lax.ppermute(give, 'pencil', swap))]
    pallas_call x2 -> x3, Pallas kernels: 5.79 us -> 5.76 us  [the longest x1 4.84 us: z_call(): vmem_call(z_kernel, (pltpu.VMEM((512, 128), F32), pltpu.VMEM((512, 128),...]
  transfers between devices with their start and end apart: 0 -> 1, of which waited for: 0 -> 1; matrix products, arithmetic and copies ran while one was open for 0% -> 0% of each run, Pallas kernels for 0% -> 0%
where the time goes in v3:
time: 99.8 us; the launch traced here: 99.6 us
  blocking collectives  88.4 us (89%)
  Pallas kernels  9.02 us (9%)
  waiting for transfers between devices  1.16 us (1%)
    all_to_all x1, blocking collectives, local(): got = lax.all_to_all(blocks, AXES, split_axis=0, concat_axis=0, tiled=True)  68.8 us
    all_to_all x1, blocking collectives, local(): lax.all_to_all(blocks.reshape(128, 4, 128), AXES, split_axis=0, concat_ax...  19.6 us
    pallas_call x1, Pallas kernels, z_call(): vmem_call(z_kernel, (pltpu.VMEM((512, 128), F32), pltpu.VMEM((512, 128),...  4.84 us
    pallas_call x1, Pallas kernels, x_call(): vmem_call(x_kernel, pltpu.VMEM((4096, 128), F32), [pltpu.VMEM((2, 2, 32,...  3.26 us
  transfers between devices with their start and end apart: 1, of which 1 were waited for; matrix products, arithmetic and copies ran while one was open for 0% of the time, Pallas kernels for 0%

profile of v3, /device:TPU:1, one launch (start us, length us, event | category | flops | bytes accessed | tf_op | source)
XLA Modules:
  0.0 99.6 jit_solution(2420888636931253479)
XLA Ops:
  0.0 3.3 %shard_map.82 = f32[4096,128]{1,0:T(8,128)S(1)} custom-call(f32[2,2,32,4096]{3,2,1,0:T(8,128)} %data.1, f32[32,256]{1,0:T(8,128)} %constant.14.clone.twist_hbm, bf16[512,256]{1,0:T(8,128)(2,1)} %constant.15.clone.high_hbm, bf16[512,256]{1,0:T(8,128)(2,1)} %constant.16.clone.low_hbm), custom_call_target="tpu_custom_call" | custom-call | tf_op jit(solution)/shard_map/pallas_call | solution.py:311
  3.3 0.0 copy-start
  3.3 0.0 copy-start.1
  3.3 0.0 copy-start.2
  3.3 0.0 copy-start.3
  3.3 68.8 %all_to_all.10 = f32[256,16,128]{2,1,0:T(8,128)S(1)} all-to-all(f32[256,16,128]{2,1,0:T(8,128)S(1)} %bitcast.4), channel_id=1, replica_groups=mesh['slab'=4,'pencil'=64] {'slab','pencil'}, dimensions={0} | all-to-all | bytes 4194304 | tf_op jit(solution)/shard_map/all_to_all | solution.py:339
  72.1 0.0 copy-done
  72.1 0.0 copy-done.1
  72.1 0.0 copy-done.2
  72.1 0.0 copy-done.3
  72.1 4.8 %shard_map.83 = (f32[512,128]{1,0:T(8,128)S(1)}, f32[512,128]{1,0:T(8,128)S(1)}) custom-call(f32[4096,128]{1,0:T(8,128)S(1)} %bitcast.5, bf16[2,256,256]{2,1,0:T(8,128)(2,1)S(1)} %copy-done, bf16[2,256,128]{2,1,0:T(8,128)(2,1)S(1)} %copy-done.3, f32[2,128,128]{2,1,0:T(8,128)S(1)} %copy-done.2, bf16[256,256]{1,0:T(8,128)(2,1)S(1)} %copy-done.1), custom_call_target="tpu_custom_call" | custom-call | tf_op jit(solution)/shard_map/pallas_call | solution.py:330
  77.0 0.9 collective-permute-start
  77.9 1.2 %collective-permute-done.got = f32[512,128]{1,0:T(8,128)S(1)} collective-permute-done((f32[512,128]{1,0:T(8,128)S(1)}, f32[512,128]{1,0:T(8,128)S(1)}, u32[]{:S(2)}, u32[]{:S(2)}) %collective-permute-start) | collective-permute-done | bytes 262176 | tf_op jit(solution)/shard_map/ppermute | solution.py:342
  79.1 0.1 shard_map.84
  79.1 19.6 %all_to_all.11 = f32[128,4,128]{2,1,0:T(4,128)S(1)} all-to-all(f32[128,4,128]{2,1,0:T(4,128)S(1)} %bitcast.6), channel_id=1, replica_groups={{0,2,4,6,8,10,12,14,16,18,20,22,24,26,28,30,32,34,36,38,40,42,44,46,48,..., dimensions={0} | all-to-all | bytes 524288 | tf_op jit(solution)/shard_map/all_to_all | solution.py:345
  98.7 0.9 shard_map.85
Async XLA Ops:
  3.3 68.8 %copy-start = (bf16[2,256,256]{2,1,0:T(8,128)(2,1)S(1)}, bf16[2,256,256]{2,1,0:T(8,128)(2,1)}, u32[]{:S(2)}) copy-start(bf16[2,256,256]{2,1,0:T(8,128)(2,1)} %constant.17.clone.first_both) | copy-start | bytes 786436
  3.3 68.8 %copy-start.1 = (bf16[256,256]{1,0:T(8,128)(2,1)S(1)}, bf16[256,256]{1,0:T(8,128)(2,1)}, u32[]{:S(2)}) copy-start(bf16[256,256]{1,0:T(8,128)(2,1)} %constant.20.clone.second_all) | copy-start | bytes 393220
  3.3 68.8 %copy-start.2 = (f32[2,128,128]{2,1,0:T(8,128)S(1)}, f32[2,128,128]{2,1,0:T(8,128)}, u32[]{:S(2)}) copy-start(f32[2,128,128]{2,1,0:T(8,128)} %constant.19.clone.twist) | copy-start | bytes 393220
  3.3 68.8 %copy-start.3 = (bf16[2,256,128]{2,1,0:T(8,128)(2,1)S(1)}, bf16[2,256,128]{2,1,0:T(8,128)(2,1)}, u32[]{:S(2)}) copy-start(bf16[2,256,128]{2,1,0:T(8,128)(2,1)} %constant.18.clone.first_low) | copy-start | bytes 393220
  77.0 2.1 %collective-permute-start = (f32[512,128]{1,0:T(8,128)S(1)}, f32[512,128]{1,0:T(8,128)S(1)}, u32[]{:S(2)}, u32[]{:S(2)}) collective-permute-start(f32[512,128]{1,0:T(8,128)S(1)} %get-tuple-element.8), channel_id=1, source_target_pairs={{0,1},{1,0},{2,3},{3,2},{4,5},{5,4},{6,7},{7,6},{8,9},{9,8},{10,11... | collective-permute-start | bytes 786440 | tf_op jit(solution)/shard_map/ppermute | solution.py:342

commit v4 on v3

--- a/solution.py
+++ b/solution.py
@@ -200,44 +200,31 @@
                     32 * near : 32 * near + 32, 128 * k : 128 * k + 128
                 ]
 
-    for pair in range(2):
-        first(0, 0, pair, pair)
-
-    def transform(slab, carry):
-        after = jnp.minimum(slab + 1, 3)
-        for y in range(2):
-            for pair in range(2):
-                first(slab if y == 0 else after, 1 - y, pair, 2 - 2 * y + pair)
-                second(slab, y, pair, 2 * y + pair)
-        return carry
-
-    lax.fori_loop(0, 4, transform, 0, unroll=True)
-
-    def render(y, carry):
+    first_half = lax.broadcasted_iota(jnp.int32, (32, 128), 1) < 64
+
+    def render(y, part):
+        rows = pl.ds(16 * part, 16)
         before, after = (y + 7) % 8, (y + 1) % 8
-        zero = jnp.zeros((32, 128), F32)
-        clear, depth, total, tilted, glow = jnp.ones((32, 128), F32), zero, zero, zero, zero
+        zero = jnp.zeros((16, 128), F32)
+        clear, depth, total, tilted, glow = jnp.ones((16, 128), F32), zero, zero, zero, zero
         for x in range(16):
-            half = field[x, y]
-            shading = 2.0 + jnp.tanh(field[x, after] - field[x, before])
+            half = field[x, y, rows]
+            shading = 2.0 + jnp.tanh(field[x, after, rows] - field[x, before, rows])
             square = half * half
-            passed = jnp.exp2(square * (-4.0 * LOG2E / N))
-            weight = (clear * shading) * (1.0 - passed)
-            clear = clear * passed
+            passed = clear * jnp.exp2(square * (-4.0 * LOG2E / N))
+            weight = (clear - passed) * shading
+            clear = passed
             depth = depth + square
             total = total + weight
             tilted = tilted + weight * jnp.tanh(3.0 * half)
             glow = glow + weight * jnp.exp2(square * (-4.0 * LOG2E))
         red = 0.25 * (total + tilted)
-        image[0, y] = red
-        image[1, y] = 0.25 * glow
-        image[2, y] = 0.5 * total - red
-        image[3, y] = depth * (4.0 / N)
-        return carry
-
-    lax.fori_loop(0, 8, render, 0)
-    first_half = lax.broadcasted_iota(jnp.int32, (32, 128), 1) < 64
-    for slab in range(4):
+        image[0, y, rows] = red
+        image[1, y, rows] = 0.25 * glow
+        image[2, y, rows] = 0.5 * total - red
+        image[3, y, rows] = depth * (4.0 / N)
+
+    def pack(slab):
         for channel in range(4):
             low, high = image[channel, 2 * slab], image[channel, 2 * slab + 1]
             mixed = (
@@ -247,6 +234,26 @@
             at = pl.ds(32 * (4 * channel + slab), 32)
             keep[at, :] = jnp.where(core == 0, mixed[0], mixed[1])
             give[at, :] = jnp.where(core == 0, mixed[1], mixed[0])
+
+    order = (7, 0, 1, 2, 3, 4, 5, 6)
+    for pair in range(2):
+        first(order[0] // 2, order[0] % 2, pair, pair)
+    for step in range(8):
+        for pair in range(2):
+            if step < 7:
+                y = order[step + 1]
+                first(y // 2, y % 2, pair, 2 - 2 * (step % 2) + pair)
+            y = order[step]
+            second(y // 2, y % 2, pair, 2 * (step % 2) + pair)
+            if step >= 3:
+                render(step - 3, pair)
+        if step in (4, 6):
+            pack(step // 2 - 2)
+    for y in (5, 6, 7):
+        for part in range(2):
+            render(y, part)
+        if y != 6:
+            pack(y // 2)
 
 
 def pair_kernel(keep, got, out):

time: 99.8 us -> 98.8 us (0.990)
  Pallas kernels: 9.02 us -> 8 us
    pallas_call x1, Pallas kernels: 4.84 us -> 3.82 us  [z_call(): vmem_call(z_kernel, (pltpu.VMEM((512, 128), F32), pltpu.VMEM((512, 128),...]
where the time goes in v4:
time: 98.8 us; the launch traced here: 98.6 us
  blocking collectives  88.4 us (89%)
  Pallas kernels  8 us (8%)
  waiting for transfers between devices  1.16 us (1%)
    all_to_all x1, blocking collectives, local(): got = lax.all_to_all(blocks, AXES, split_axis=0, concat_axis=0, tiled=True)  68.8 us
    all_to_all x1, blocking collectives, local(): lax.all_to_all(blocks.reshape(128, 4, 128), AXES, split_axis=0, concat_ax...  19.6 us
    pallas_call x1, Pallas kernels, z_call(): vmem_call(z_kernel, (pltpu.VMEM((512, 128), F32), pltpu.VMEM((512, 128),...  3.82 us
    pallas_call x1, Pallas kernels, x_call(): vmem_call(x_kernel, pltpu.VMEM((4096, 128), F32), [pltpu.VMEM((2, 2, 32,...  3.26 us
  transfers between devices with their start and end apart: 1, of which 1 were waited for; matrix products, arithmetic and copies ran while one was open for 0% of the time, Pallas kernels for 0%

profile of v4, /device:TPU:1, one launch (start us, length us, event | category | flops | bytes accessed | tf_op | source)
XLA Modules:
  0.0 98.6 jit_solution(13635602877293135256)
XLA Ops:
  0.0 3.3 %shard_map.82 = f32[4096,128]{1,0:T(8,128)S(1)} custom-call(f32[2,2,32,4096]{3,2,1,0:T(8,128)} %data.1, f32[32,256]{1,0:T(8,128)} %constant.14.clone.twist_hbm, bf16[512,256]{1,0:T(8,128)(2,1)} %constant.15.clone.high_hbm, bf16[512,256]{1,0:T(8,128)(2,1)} %constant.16.clone.low_hbm), custom_call_target="tpu_custom_call" | custom-call | tf_op jit(solution)/shard_map/pallas_call | solution.py:318
  3.3 0.0 copy-start
  3.3 0.0 copy-start.1
  3.3 0.0 copy-start.2
  3.3 0.0 copy-start.3
  3.3 68.8 %all_to_all.10 = f32[256,16,128]{2,1,0:T(8,128)S(1)} all-to-all(f32[256,16,128]{2,1,0:T(8,128)S(1)} %bitcast.4), channel_id=1, replica_groups=mesh['slab'=4,'pencil'=64] {'slab','pencil'}, dimensions={0} | all-to-all | bytes 4194304 | tf_op jit(solution)/shard_map/all_to_all | solution.py:346
  72.1 0.0 copy-done
  72.1 0.0 copy-done.1
  72.1 0.0 copy-done.2
  72.1 0.0 copy-done.3
  72.1 3.8 %shard_map.83 = (f32[512,128]{1,0:T(8,128)S(1)}, f32[512,128]{1,0:T(8,128)S(1)}) custom-call(f32[4096,128]{1,0:T(8,128)S(1)} %bitcast.5, bf16[2,256,256]{2,1,0:T(8,128)(2,1)S(1)} %copy-done, bf16[2,256,128]{2,1,0:T(8,128)(2,1)S(1)} %copy-done.3, f32[2,128,128]{2,1,0:T(8,128)S(1)} %copy-done.2, bf16[256,256]{1,0:T(8,128)(2,1)S(1)} %copy-done.1), custom_call_target="tpu_custom_call" | custom-call | tf_op jit(solution)/shard_map/pallas_call | solution.py:337
  76.0 0.9 collective-permute-start
  76.9 1.2 %collective-permute-done.got = f32[512,128]{1,0:T(8,128)S(1)} collective-permute-done((f32[512,128]{1,0:T(8,128)S(1)}, f32[512,128]{1,0:T(8,128)S(1)}, u32[]{:S(2)}, u32[]{:S(2)}) %collective-permute-start) | collective-permute-done | bytes 262176 | tf_op jit(solution)/shard_map/ppermute | solution.py:349
  78.1 0.1 shard_map.84
  78.1 19.6 %all_to_all.11 = f32[128,4,128]{2,1,0:T(4,128)S(1)} all-to-all(f32[128,4,128]{2,1,0:T(4,128)S(1)} %bitcast.6), channel_id=1, replica_groups={{0,2,4,6,8,10,12,14,16,18,20,22,24,26,28,30,32,34,36,38,40,42,44,46,48,..., dimensions={0} | all-to-all | bytes 524288 | tf_op jit(solution)/shard_map/all_to_all | solution.py:352
  97.7 0.9 shard_map.85
Async XLA Ops:
  3.3 68.8 %copy-start = (bf16[2,256,256]{2,1,0:T(8,128)(2,1)S(1)}, bf16[2,256,256]{2,1,0:T(8,128)(2,1)}, u32[]{:S(2)}) copy-start(bf16[2,256,256]{2,1,0:T(8,128)(2,1)} %constant.17.clone.first_both) | copy-start | bytes 786436
  3.3 68.8 %copy-start.1 = (bf16[256,256]{1,0:T(8,128)(2,1)S(1)}, bf16[256,256]{1,0:T(8,128)(2,1)}, u32[]{:S(2)}) copy-start(bf16[256,256]{1,0:T(8,128)(2,1)} %constant.20.clone.second_all) | copy-start | bytes 393220
  3.3 68.8 %copy-start.2 = (f32[2,128,128]{2,1,0:T(8,128)S(1)}, f32[2,128,128]{2,1,0:T(8,128)}, u32[]{:S(2)}) copy-start(f32[2,128,128]{2,1,0:T(8,128)} %constant.19.clone.twist) | copy-start | bytes 393220
  3.3 68.8 %copy-start.3 = (bf16[2,256,128]{2,1,0:T(8,128)(2,1)S(1)}, bf16[2,256,128]{2,1,0:T(8,128)(2,1)}, u32[]{:S(2)}) copy-start(bf16[2,256,128]{2,1,0:T(8,128)(2,1)} %constant.18.clone.first_low) | copy-start | bytes 393220
  76.0 2.1 %collective-permute-start = (f32[512,128]{1,0:T(8,128)S(1)}, f32[512,128]{1,0:T(8,128)S(1)}, u32[]{:S(2)}, u32[]{:S(2)}) collective-permute-start(f32[512,128]{1,0:T(8,128)S(1)} %get-tuple-element.8), channel_id=1, source_target_pairs={{0,1},{1,0},{2,3},{3,2},{4,5},{5,4},{6,7},{7,6},{8,9},{9,8},{10,11... | collective-permute-start | bytes 786440 | tf_op jit(solution)/shard_map/ppermute | solution.py:349

commit v5 on v4

--- a/solution.py
+++ b/solution.py
@@ -200,7 +200,6 @@
                     32 * near : 32 * near + 32, 128 * k : 128 * k + 128
                 ]
 
-    first_half = lax.broadcasted_iota(jnp.int32, (32, 128), 1) < 64
 
     def render(y, part):
         rows = pl.ds(16 * part, 16)
@@ -226,14 +225,9 @@
 
     def pack(slab):
         for channel in range(4):
-            low, high = image[channel, 2 * slab], image[channel, 2 * slab + 1]
-            mixed = (
-                jnp.where(first_half, low, pltpu.roll(high, 64, 1)),
-                jnp.where(first_half, pltpu.roll(low, 64, 1), high),
-            )
             at = pl.ds(32 * (4 * channel + slab), 32)
-            keep[at, :] = jnp.where(core == 0, mixed[0], mixed[1])
-            give[at, :] = jnp.where(core == 0, mixed[1], mixed[0])
+            keep[at, :] = image[channel, 2 * slab + core]
+            give[at, :] = image[channel, 2 * slab + 1 - core]
 
     order = (7, 0, 1, 2, 3, 4, 5, 6)
     for pair in range(2):
@@ -258,40 +252,49 @@
 
 def pair_kernel(keep, got, out):
     own_first = lax.axis_index("pencil") % 2 == lax.axis_index("slab") // 2
+    first_half = lax.broadcasted_iota(jnp.int32, (32, 128), 1) < 64
     for slab in range(4):
-        own = [keep[pl.ds(32 * (4 * channel + slab), 32), :] for channel in range(4)]
-        other = [got[pl.ds(32 * (4 * channel + slab), 32), :] for channel in range(4)]
+        rows = [pl.ds(32 * (4 * channel + slab), 32) for channel in range(4)]
+        own = [keep[at, :] for at in rows]
+        other = [got[at, :] for at in rows]
         clear = jnp.exp(-jnp.where(own_first, own[3], other[3]))
-        for channel in range(4):
-            if channel == 3:
-                value = own[3] + other[3]
-            else:
-                front = jnp.where(own_first, own[channel], other[channel])
-                back = jnp.where(own_first, other[channel], own[channel])
-                value = front + clear * back
-            out[pl.ds(128 * slab + channel, 32, stride=4), :] = value
+        merged = []
+        for channel in range(3):
+            front = jnp.where(own_first, own[channel], other[channel])
+            back = jnp.where(own_first, other[channel], own[channel])
+            merged.append(front + clear * back)
+        merged.append(own[3] + other[3])
+        for row in range(2):
+            low, high = merged[2 * row], merged[2 * row + 1]
+            mixed = (
+                jnp.where(first_half, low, pltpu.roll(high, 64, 1)),
+                jnp.where(first_half, pltpu.roll(low, 64, 1), high),
+            )
+            for core in range(2):
+                out[pl.ds(128 * slab + 2 * core + row, 32, stride=4), :] = mixed[core]
 
 
 def blend_kernel(got, out):
-    depth = got[pl.ds(3, 128, stride=4), :]
     row = lax.broadcasted_iota(jnp.int32, (128, 128), 0)
     col = lax.broadcasted_iota(jnp.int32, (128, 128), 1)
     rank = jnp.where(row < 64, row, 191 - row)
     earlier = (jnp.where(col < 64, col, 191 - col) < rank).astype(BF16)
-    high = depth.astype(BF16)
-    rest = depth - high.astype(F32)
-    middle = rest.astype(BF16)
-    low = (rest - middle.astype(F32)).astype(BF16)
-    before = straight(earlier, high) + straight(earlier, middle) + straight(earlier, low)
-    clear = jnp.exp(-before)
-    rows = [
-        jnp.sum(clear * got[pl.ds(channel, 128, stride=4), :], axis=0, keepdims=True)
-        for channel in range(3)
-    ]
-    rows.append(1.0 - jnp.exp(-jnp.sum(depth, axis=0, keepdims=True)))
-    for channel in range(4):
-        for y in range(2):
-            out[channel, pl.ds(y, 1), :] = rows[channel][:, 64 * y : 64 * y + 64]
+    for y in range(2):
+        red_green = got[pl.ds(2 * y, 128, stride=4), :]
+        blue_depth = got[pl.ds(2 * y + 1, 128, stride=4), :]
+        depth = jnp.where(col < 64, pltpu.roll(blue_depth, 64, 1), blue_depth)
+        high = depth.astype(BF16)
+        rest = depth - high.astype(F32)
+        middle = rest.astype(BF16)
+        low = (rest - middle.astype(F32)).astype(BF16)
+        before = straight(earlier, high) + straight(earlier, middle) + straight(earlier, low)
+        clear = jnp.exp(-before)
+        mixed = jnp.sum(clear * red_green, axis=0, keepdims=True)
+        out[0, pl.ds(y, 1), :] = mixed[:, :64]
+        out[1, pl.ds(y, 1), :] = mixed[:, 64:]
+        out[2, pl.ds(y, 1), :] = jnp.sum(clear * blue_depth, axis=0, keepdims=True)[:, :64]
+        opacity = 1.0 - jnp.exp(-jnp.sum(depth, axis=0, keepdims=True))
+        out[3, pl.ds(y, 1), :] = opacity[:, :64]
 
 
 def vmem_call(kernel, out_type, scratch=(), in_specs=None):
@@ -348,14 +351,8 @@
     swap = [(i, i ^ 1) for i in range(lax.axis_size("pencil"))]
     other = near(lax.ppermute(give, "pencil", swap))
     blocks = vmem_call(pair_kernel, pltpu.VMEM((512, 128), F32))(near(keep), other)
-    same_core = [[2 * i + core for i in range(128)] for core in range(2)]
     got = lax.all_to_all(
-        blocks.reshape(128, 4, 128),
-        AXES,
-        split_axis=0,
-        concat_axis=0,
-        axis_index_groups=same_core,
-        tiled=True,
+        blocks.reshape(256, 2, 128), AXES, split_axis=0, concat_axis=0, tiled=True
     )
     out_type = jax.ShapeDtypeStruct((4, 2, 64), F32)
     return vmem_call(blend_kernel, out_type)(near(got.reshape(512, 128)))

time: 98.8 us -> 101 us (1.022)
  blocking collectives: 88.4 us -> 90 us
    all_to_all x1, blocking collectives: 19.6 us -> 21.2 us  [local(): lax.all_to_all(blocks.reshape(256, 2, 128), AXES, split_axis=0, concat_ax...]
where the time goes in v5:
time: 101 us; the launch traced here: 100 us
  blocking collectives  90 us (89%)
  Pallas kernels  8.22 us (8%)
  waiting for transfers between devices  1.16 us (1%)
    all_to_all x1, blocking collectives, local(): got = lax.all_to_all(blocks, AXES, split_axis=0, concat_axis=0, tiled=True)  68.8 us
    all_to_all x1, blocking collectives, local(): lax.all_to_all(blocks.reshape(256, 2, 128), AXES, split_axis=0, concat_ax...  21.2 us
    pallas_call x1, Pallas kernels, z_call(): vmem_call(z_kernel, (pltpu.VMEM((512, 128), F32), pltpu.VMEM((512, 128),...  3.83 us
    pallas_call x1, Pallas kernels, x_call(): vmem_call(x_kernel, pltpu.VMEM((4096, 128), F32), [pltpu.VMEM((2, 2, 32,...  3.26 us
  transfers between devices with their start and end apart: 1, of which 1 were waited for; matrix products, arithmetic and copies ran while one was open for 0% of the time, Pallas kernels for 0%

profile of v5, /device:TPU:1, one launch (start us, length us, event | category | flops | bytes accessed | tf_op | source)
XLA Modules:
  0.0 100.4 jit_solution(2119487112817855663)
XLA Ops:
  0.0 3.3 %shard_map.82 = f32[4096,128]{1,0:T(8,128)S(1)} custom-call(f32[2,2,32,4096]{3,2,1,0:T(8,128)} %data.1, f32[32,256]{1,0:T(8,128)} %constant.14.clone.twist_hbm, bf16[512,256]{1,0:T(8,128)(2,1)} %constant.15.clone.high_hbm, bf16[512,256]{1,0:T(8,128)(2,1)} %constant.16.clone.low_hbm), custom_call_target="tpu_custom_call" | custom-call | tf_op jit(solution)/shard_map/pallas_call | solution.py:321
  3.3 0.0 copy-start
  3.3 0.0 copy-start.1
  3.3 0.0 copy-start.2
  3.3 0.0 copy-start.3
  3.3 68.8 %all_to_all.10 = f32[256,16,128]{2,1,0:T(8,128)S(1)} all-to-all(f32[256,16,128]{2,1,0:T(8,128)S(1)} %bitcast.4), channel_id=1, replica_groups=mesh['slab'=4,'pencil'=64] {'slab','pencil'}, dimensions={0} | all-to-all | bytes 4194304 | tf_op jit(solution)/shard_map/all_to_all | solution.py:349
  72.1 0.0 copy-done
  72.1 0.0 copy-done.1
  72.1 0.0 copy-done.2
  72.1 0.0 copy-done.3
  72.1 3.8 %shard_map.83 = (f32[512,128]{1,0:T(8,128)S(1)}, f32[512,128]{1,0:T(8,128)S(1)}) custom-call(f32[4096,128]{1,0:T(8,128)S(1)} %bitcast.5, bf16[2,256,256]{2,1,0:T(8,128)(2,1)S(1)} %copy-done, bf16[2,256,128]{2,1,0:T(8,128)(2,1)S(1)} %copy-done.3, f32[2,128,128]{2,1,0:T(8,128)S(1)} %copy-done.2, bf16[256,256]{1,0:T(8,128)(2,1)S(1)} %copy-done.1), custom_call_target="tpu_custom_call" | custom-call | tf_op jit(solution)/shard_map/pallas_call | solution.py:340
  76.0 0.9 collective-permute-start
  76.9 1.2 %collective-permute-done.got = f32[512,128]{1,0:T(8,128)S(1)} collective-permute-done((f32[512,128]{1,0:T(8,128)S(1)}, f32[512,128]{1,0:T(8,128)S(1)}, u32[]{:S(2)}, u32[]{:S(2)}) %collective-permute-start) | collective-permute-done | bytes 262176 | tf_op jit(solution)/shard_map/ppermute | solution.py:352
  78.1 0.2 shard_map.84
  78.2 21.2 %all_to_all.11 = f32[256,2,128]{2,1,0:T(2,128)S(1)} all-to-all(f32[256,2,128]{2,1,0:T(2,128)S(1)} %bitcast.6), channel_id=1, replica_groups=mesh['slab'=4,'pencil'=64] {'slab','pencil'}, dimensions={0} | all-to-all | bytes 524288 | tf_op jit(solution)/shard_map/all_to_all | solution.py:354
  99.4 1.0 shard_map.85
Async XLA Ops:
  3.3 68.8 %copy-start = (bf16[2,256,256]{2,1,0:T(8,128)(2,1)S(1)}, bf16[2,256,256]{2,1,0:T(8,128)(2,1)}, u32[]{:S(2)}) copy-start(bf16[2,256,256]{2,1,0:T(8,128)(2,1)} %constant.17.clone.first_both) | copy-start | bytes 786436
  3.3 68.8 %copy-start.1 = (bf16[256,256]{1,0:T(8,128)(2,1)S(1)}, bf16[256,256]{1,0:T(8,128)(2,1)}, u32[]{:S(2)}) copy-start(bf16[256,256]{1,0:T(8,128)(2,1)} %constant.20.clone.second_all) | copy-start | bytes 393220
  3.3 68.8 %copy-start.2 = (f32[2,128,128]{2,1,0:T(8,128)S(1)}, f32[2,128,128]{2,1,0:T(8,128)}, u32[]{:S(2)}) copy-start(f32[2,128,128]{2,1,0:T(8,128)} %constant.19.clone.twist) | copy-start | bytes 393220
  3.3 68.8 %copy-start.3 = (bf16[2,256,128]{2,1,0:T(8,128)(2,1)S(1)}, bf16[2,256,128]{2,1,0:T(8,128)(2,1)}, u32[]{:S(2)}) copy-start(bf16[2,256,128]{2,1,0:T(8,128)(2,1)} %constant.18.clone.first_low) | copy-start | bytes 393220
  76.0 2.1 %collective-permute-start = (f32[512,128]{1,0:T(8,128)S(1)}, f32[512,128]{1,0:T(8,128)S(1)}, u32[]{:S(2)}, u32[]{:S(2)}) collective-permute-start(f32[512,128]{1,0:T(8,128)S(1)} %get-tuple-element.8), channel_id=1, source_target_pairs={{0,1},{1,0},{2,3},{3,2},{4,5},{5,4},{6,7},{7,6},{8,9},{9,8},{10,11... | collective-permute-start | bytes 786440 | tf_op jit(solution)/shard_map/ppermute | solution.py:352

commit v6 on v4

--- a/solution.py
+++ b/solution.py
@@ -96,8 +96,8 @@
             )
     copies.append(pltpu.make_async_copy(high_hbm, high_w, sems.at[5]))
     copies.append(pltpu.make_async_copy(low_hbm, low_w, sems.at[6]))
-    for copy in copies:
-        copy.start()
+    for index in (1, 0, 2, 5, 6, 3, 4):
+        copies[index].start()
 
     def stage(y, half, tile):
         rows, lanes = pl.ds(16 * half, 16), pl.ds(128 * tile, 128)
@@ -141,12 +141,14 @@
         copies[1 + half].wait()
         for tile in range(2):
             stage(0, half, tile)
-    for copy in copies[3:]:
-        copy.wait()
+    for index in (5, 6, 3):
+        copies[index].wait()
     for pair in range(2):
         send(0, pair)
-        for tile in range(2):
-            stage(1, pair, tile)
+        stage(1, 0, pair)
+    copies[4].wait()
+    for tile in range(2):
+        stage(1, 1, tile)
     for pair in range(2):
         send(1, pair)
 

time: 98.8 us -> 98.7 us (level)
  no operation moved by 1% of the time
where the time goes in v6:
time: 98.7 us; the launch traced here: 98.5 us
  blocking collectives  88.4 us (90%)
  Pallas kernels  7.89 us (8%)
  waiting for transfers between devices  1.16 us (1%)
    all_to_all x1, blocking collectives, local(): got = lax.all_to_all(blocks, AXES, split_axis=0, concat_axis=0, tiled=True)  68.8 us
    all_to_all x1, blocking collectives, local(): lax.all_to_all(blocks.reshape(128, 4, 128), AXES, split_axis=0, concat_ax...  19.6 us
    pallas_call x1, Pallas kernels, z_call(): vmem_call(z_kernel, (pltpu.VMEM((512, 128), F32), pltpu.VMEM((512, 128),...  3.82 us
    pallas_call x1, Pallas kernels, x_call(): vmem_call(x_kernel, pltpu.VMEM((4096, 128), F32), [pltpu.VMEM((2, 2, 32,...  3.15 us
  transfers between devices with their start and end apart: 1, of which 1 were waited for; matrix products, arithmetic and copies ran while one was open for 0% of the time, Pallas kernels for 0%

profile of v6, /device:TPU:1, one launch (start us, length us, event | category | flops | bytes accessed | tf_op | source)
XLA Modules:
  0.0 98.5 jit_solution(13792607864711352229)
XLA Ops:
  0.0 3.1 %shard_map.82 = f32[4096,128]{1,0:T(8,128)S(1)} custom-call(f32[2,2,32,4096]{3,2,1,0:T(8,128)} %data.1, f32[32,256]{1,0:T(8,128)} %constant.14.clone.twist_hbm, bf16[512,256]{1,0:T(8,128)(2,1)} %constant.15.clone.high_hbm, bf16[512,256]{1,0:T(8,128)(2,1)} %constant.16.clone.low_hbm), custom_call_target="tpu_custom_call" | custom-call | tf_op jit(solution)/shard_map/pallas_call | solution.py:320
  3.2 0.0 copy-start
  3.2 0.0 copy-start.1
  3.2 0.0 copy-start.2
  3.2 0.0 copy-start.3
  3.2 68.8 %all_to_all.10 = f32[256,16,128]{2,1,0:T(8,128)S(1)} all-to-all(f32[256,16,128]{2,1,0:T(8,128)S(1)} %bitcast.4), channel_id=1, replica_groups=mesh['slab'=4,'pencil'=64] {'slab','pencil'}, dimensions={0} | all-to-all | bytes 4194304 | tf_op jit(solution)/shard_map/all_to_all | solution.py:348
  72.0 0.0 copy-done
  72.0 0.0 copy-done.1
  72.0 0.0 copy-done.2
  72.0 0.0 copy-done.3
  72.0 3.8 %shard_map.83 = (f32[512,128]{1,0:T(8,128)S(1)}, f32[512,128]{1,0:T(8,128)S(1)}) custom-call(f32[4096,128]{1,0:T(8,128)S(1)} %bitcast.5, bf16[2,256,256]{2,1,0:T(8,128)(2,1)S(1)} %copy-done, bf16[2,256,128]{2,1,0:T(8,128)(2,1)S(1)} %copy-done.3, f32[2,128,128]{2,1,0:T(8,128)S(1)} %copy-done.2, bf16[256,256]{1,0:T(8,128)(2,1)S(1)} %copy-done.1), custom_call_target="tpu_custom_call" | custom-call | tf_op jit(solution)/shard_map/pallas_call | solution.py:339
  75.8 0.9 collective-permute-start
  76.8 1.2 %collective-permute-done.got = f32[512,128]{1,0:T(8,128)S(1)} collective-permute-done((f32[512,128]{1,0:T(8,128)S(1)}, f32[512,128]{1,0:T(8,128)S(1)}, u32[]{:S(2)}, u32[]{:S(2)}) %collective-permute-start) | collective-permute-done | bytes 262176 | tf_op jit(solution)/shard_map/ppermute | solution.py:351
  77.9 0.1 shard_map.84
  78.0 19.6 %all_to_all.11 = f32[128,4,128]{2,1,0:T(4,128)S(1)} all-to-all(f32[128,4,128]{2,1,0:T(4,128)S(1)} %bitcast.6), channel_id=1, replica_groups={{0,2,4,6,8,10,12,14,16,18,20,22,24,26,28,30,32,34,36,38,40,42,44,46,48,..., dimensions={0} | all-to-all | bytes 524288 | tf_op jit(solution)/shard_map/all_to_all | solution.py:354
  97.6 0.9 shard_map.85
Async XLA Ops:
  3.2 68.8 %copy-start = (bf16[2,256,256]{2,1,0:T(8,128)(2,1)S(1)}, bf16[2,256,256]{2,1,0:T(8,128)(2,1)}, u32[]{:S(2)}) copy-start(bf16[2,256,256]{2,1,0:T(8,128)(2,1)} %constant.17.clone.first_both) | copy-start | bytes 786436
  3.2 68.8 %copy-start.1 = (bf16[256,256]{1,0:T(8,128)(2,1)S(1)}, bf16[256,256]{1,0:T(8,128)(2,1)}, u32[]{:S(2)}) copy-start(bf16[256,256]{1,0:T(8,128)(2,1)} %constant.20.clone.second_all) | copy-start | bytes 393220
  3.2 68.8 %copy-start.2 = (f32[2,128,128]{2,1,0:T(8,128)S(1)}, f32[2,128,128]{2,1,0:T(8,128)}, u32[]{:S(2)}) copy-start(f32[2,128,128]{2,1,0:T(8,128)} %constant.19.clone.twist) | copy-start | bytes 393220
  3.2 68.8 %copy-start.3 = (bf16[2,256,128]{2,1,0:T(8,128)(2,1)S(1)}, bf16[2,256,128]{2,1,0:T(8,128)(2,1)}, u32[]{:S(2)}) copy-start(bf16[2,256,128]{2,1,0:T(8,128)(2,1)} %constant.18.clone.first_low) | copy-start | bytes 393220
  75.8 2.1 %collective-permute-start = (f32[512,128]{1,0:T(8,128)S(1)}, f32[512,128]{1,0:T(8,128)S(1)}, u32[]{:S(2)}, u32[]{:S(2)}) collective-permute-start(f32[512,128]{1,0:T(8,128)S(1)} %get-tuple-element.8), channel_id=1, source_target_pairs={{0,1},{1,0},{2,3},{3,2},{4,5},{5,4},{6,7},{7,6},{8,9},{9,8},{10,11... | collective-permute-start | bytes 786440 | tf_op jit(solution)/shard_map/ppermute | solution.py:351
